TPU v7x, 128 devices: a whole 4x4x4 slice. The times are simulated.
128 devices in a mesh: occ: 8 (over x, core), vir: 16 (over y, z).
Axes of the slice: x: 4, y: 4, z: 4, core: 2. Of those that a mesh axis runs over, the one named last changes fastest.
Arguments:
- amplitudes: bfloat16 [8, 2, 4096, 4096], P('occ', None, None, 'vir'), may hold values from -6 to 6
- coulomb: bfloat16 [8, 2, 4096, 4096], P('occ', None, None, 'vir'), may hold values from -6 to 6
- ladder_tiles: bfloat16 [256, 128, 128], P('vir'), may hold values from -0.1875 to 0.1875
- cycle_tiles: bfloat16 [256, 128, 128], P('vir'), may hold values from -0.25 to 0.25
- ladder_screen: int32 [32, 8], replicated, may hold values from 0 to 31, as said below
- tile_slot: int32 [256], replicated, may hold values from 0 to 255, each once
- cycle_screen: int32 [64, 4], replicated, may hold values from 0 to 63, as said below
- cycle_rows: int32 [32, 48], replicated, may hold values from 0 to 63, as said below
- cycle_count: int32 [32], replicated, may hold values from 1 to 48, 1024 in all
- slab_occ: int32 [8], replicated, may hold values from 0 to 399
- window_occ: int32 [2], replicated, may hold values from 0 to 399
- occ_energy: float32 [400], replicated, may hold values from -3 to -0.5
- vir_energy: float32 [4096], replicated, may hold values from 0.4 to 4
Outputs:
- updated: bfloat16 [8, 2, 4096, 4096], P('occ', None, None, 'vir')
Inputs may be any that keep to these rules, and one draw needn't show every extreme that they name: `ladder_screen`: each row names 8 different tiles. `cycle_screen`: each row names 4 different row tiles. `cycle_rows`: each row names 48 different block columns; the first cycle_count of them are used. `cycle_count`: the counts sum to exactly 1024, and the largest is exactly 48.
All inputs are finite; a program needn't handle non-finite values.
Results may differ from a plain program's by a relative error of at most 0.003.
Values may be sent and summed in bfloat16 or wider, within the bound.
No kernel may reach another device: no remote copies, remote signals or barrier semaphores. Data moves between devices by JAX's collectives and lax.ppermute only.
A program may use at most 192 MiB of HBM per device.

v0:
```python
import math
import jax
import jax.numpy as jnp
from jax import lax
from jax.sharding import PartitionSpec as P


def body(
    amplitudes,
    coulomb,
    ladder_tiles,
    cycle_tiles,
    ladder_screen,
    tile_slot,
    cycle_screen,
    cycle_rows,
    cycle_count,
    slab_occ,
    window_occ,
    occ_energy,
    vir_energy,
):
    occ_count = lax.axis_size("occ")
    vir_count = lax.axis_size("vir")
    dev_count = occ_count * vir_count
    slab_rows, window, width_all, block_cols = amplitudes.shape
    tile_side = ladder_tiles.shape[1]
    tile_count = width_all // tile_side
    ladder_keep = ladder_screen.shape[1]
    cycle_keep = cycle_screen.shape[1]
    column_tiles = cycle_screen.shape[0]
    rows_here = width_all // dev_count
    slab_all = slab_rows * occ_count
    all_ladder, all_cycle = (
        lax.all_gather(ladder_tiles, "vir", axis=0, tiled=True),
        lax.all_gather(cycle_tiles, "vir", axis=0, tiled=True),
    )
    front, inner = (1, rows_here)
    split = amplitudes.reshape(slab_rows, window, front, occ_count, vir_count, inner, block_cols)
    flat = split.reshape(1, slab_rows, window, front, dev_count, inner, block_cols)
    moved = lax.all_to_all(flat, ("occ", "vir"), split_axis=4, concat_axis=0, tiled=True)
    moved = moved.reshape(occ_count, vir_count, slab_rows, window, front, inner, block_cols)
    moved = moved.transpose(0, 2, 3, 4, 5, 1, 6)
    cycle_amp = moved.reshape(slab_all, window, front * inner, width_all)
    extent = slab_rows * window * block_cols
    arranged = amplitudes.transpose(2, 0, 1, 3).reshape(tile_count, tile_side, extent)
    slots = tile_slot.reshape(tile_count, ladder_keep)
    group = math.gcd(tile_count, 8)

    def ladder_block(start):
        screen_part = lax.dynamic_slice_in_dim(ladder_screen, start, group, 0)
        slot_part = lax.dynamic_slice_in_dim(slots, start, group, 0)
        picked_rows = arranged[screen_part]
        weights = all_ladder[slot_part]
        return jnp.einsum(
            "akrc,akce->are", weights, picked_rows, preferred_element_type=jnp.float32
        )

    starts = jnp.arange(0, tile_count, group, dtype=jnp.int32)
    total = lax.map(ladder_block, starts)
    ladder = total.reshape(width_all, slab_rows, window, block_cols).transpose(1, 2, 0, 3)
    source = cycle_amp.reshape(slab_all, window, front, inner, tile_count, tile_side)
    source = source.transpose(1, 4, 2, 0, 3, 5).reshape(
        window * tile_count, front, slab_all * inner, tile_side
    )
    cycle_sel = all_cycle.reshape(column_tiles, cycle_keep, tile_side, tile_side)
    device = lax.axis_index("occ") * vir_count + lax.axis_index("vir")
    my_tile = device * rows_here // tile_side
    columns = lax.dynamic_index_in_dim(cycle_rows, my_tile, 0, keepdims=False)
    used = lax.dynamic_index_in_dim(cycle_count, my_tile, 0, keepdims=False)
    valid = jnp.arange(columns.shape[0], dtype=jnp.int32) < used
    picked = source[cycle_screen[columns], 0]
    part = jnp.einsum(
        "emrc,emcb->erb", picked, cycle_sel[columns], preferred_element_type=jnp.float32
    )
    part = jnp.where(valid[:, None, None], part, 0.0)
    placed = (
        jnp.zeros((column_tiles, slab_all * inner, tile_side), jnp.float32).at[columns].add(part)
    )
    cycle_cols = placed.reshape(column_tiles, front, slab_all * inner, tile_side)
    cycle_cols = cycle_cols.astype(jnp.bfloat16).reshape(
        window, tile_count, front, slab_all, inner, tile_side
    )
    cycle_view = cycle_cols.transpose(3, 0, 2, 4, 1, 5).reshape(
        slab_all, window, front * inner, width_all
    )
    shaped = cycle_view.reshape(occ_count, slab_rows, window, front, inner, vir_count, block_cols)
    shaped = shaped.transpose(0, 5, 1, 2, 3, 4, 6).reshape(
        dev_count, slab_rows, window, front, 1, inner, block_cols
    )
    back = lax.all_to_all(shaped, ("occ", "vir"), split_axis=0, concat_axis=4, tiled=True)
    cycle = back.reshape(slab_rows, window, width_all, block_cols)
    occ_total = occ_energy.shape[0]
    orbital_ids = jnp.arange(occ_total, dtype=jnp.int32)
    my_slab = lax.dynamic_slice_in_dim(slab_occ, lax.axis_index("occ") * slab_rows, slab_rows)
    energy_i = jnp.sum(
        jnp.where(my_slab[:, None] == orbital_ids[None, :], occ_energy[None, :], 0.0), axis=1
    )
    energy_j = jnp.sum(
        jnp.where(window_occ[:, None] == orbital_ids[None, :], occ_energy[None, :], 0.0), axis=1
    )
    energy_b = lax.dynamic_slice_in_dim(vir_energy, lax.axis_index("vir") * block_cols, block_cols)
    denominator = (
        vir_energy[None, None, :, None]
        + energy_b[None, None, None, :]
        - energy_i[:, None, None, None]
        - energy_j[None, :, None, None]
    )
    value = coulomb.astype(jnp.float32) + ladder + cycle.astype(jnp.float32)
    return (value / denominator).astype(jnp.bfloat16)


def solution(mesh):
    return jax.shard_map(
        body,
        mesh=mesh,
        in_specs=(
            P("occ", None, None, "vir"),
            P("occ", None, None, "vir"),
            P("vir", None, None),
            P("vir", None, None),
            P(),
            P(),
            P(),
            P(),
            P(),
            P(),
            P(),
            P(),
            P(),
        ),
        out_specs=P("occ", None, None, "vir"),
        check_vma=False,
    )
```

profile of v0, /device:TPU:1, one launch (start us, length us, event | category | flops | bytes accessed | tf_op | source)
XLA Modules:
  0.0 347.0 jit_solution(11415876466510590525)
XLA Ops:
  6.5 0.7 all-gather.5.cloned.1.call-update
  7.3 0.7 all-gather.3.cloned.1.call-update
  8.0 4.8 %copy.67 = bf16[1,1,2,1,128,32,256]{6,5,2,3,1,0,4:T(8,128)(2,1)} copy(bf16[1,1,2,1,128,32,256]{6,5,4,2,3,1,0:T(8,128)(2,1)} %bitcast.87) | data formatting | bytes 8388608 | tf_op jit(solution)/shard_map/reshape;reshape | solution.py:40
  12.9 11.9 %all-to-all-start = ((bf16[1,1,2,1,128,32,256]{6,5,2,3,1,0,4:T(8,128)(2,1)}), bf16[1,1,2,1,128,32,256]{6,5,2,3,1,0,4:T(8,128)(2,1)}, u32[]{:S(2)}, u32[]{:S(2)}) async-start(bf16[1,1,2,1,128,32,256]{6,5,2,3,1,0,4:T(8,128)(2,1)} %copy.67), calls=%async_computation | async-start | bytes 8388608 | tf_op jit(solution)/shard_map/all_to_all | solution.py:41
  24.9 0.1 copy.70
  25.0 0.6 dynamic_slice.25
  25.6 0.7 fusion.6
  26.3 0.6 gather_fusion.2
  26.9 0.1 reshape.181
  27.0 0.1 reshape.147
  27.1 10.1 %copy.64 = bf16[4096,1,2,256]{3,2,0,1:T(2,128)(2,1)} copy(bf16[4096,1,2,256]{3,0,2,1:T(8,128)(2,1)} %bitcast.88) | data formatting | bytes 8388608 | tf_op jit(solution)/shard_map/transpose | solution.py:46
  37.1 7.6 %reshape.148 = bf16[32,128,512]{2,1,0:T(8,128)(2,1)} reshape(bf16[4096,1,2,256]{3,2,0,1:T(2,128)(2,1)} %copy.64) | data formatting | bytes 8388608 | tf_op jit(solution)/shard_map/reshape | solution.py:46
  44.8 6.5 %copy.63 = bf16[1,2,4096,256]{2,3,1,0:T(8,128)(2,1)} copy(bf16[1,2,4096,256]{3,2,1,0:T(8,128)(2,1)} %param.16) | data formatting | bytes 8388608 | tf_op args[1]
  51.3 0.6 dynamic_slice.27
  52.0 0.6 iota_compare_fusion.1
  52.6 1.3 select_reduce_fusion
  53.9 0.2 fusion.5
  54.1 3.1 add_subtract_fusion
  57.3 24.8 %all-to-all-done = bf16[1,1,2,1,128,32,256]{6,5,2,3,1,0,4:T(8,128)(2,1)} async-done(((bf16[1,1,2,1,128,32,256]{6,5,2,3,1,0,4:T(8,128)(2,1)}), bf16[1,1,2,1,128,32,256]{6,5,2,3,1,0,4:T(8,128)(2,1)}, u32[]{:S(2)}, u32[]{:S(2)}) %all-to-all-start) | async-done | bytes 4194336 | tf_op jit(solution)/shard_map/all_to_all | solution.py:41
  82.1 7.1 %copy.68 = bf16[8,1,2,1,32,16,256]{6,5,4,2,0,3,1:T(8,128)(2,1)} copy(bf16[8,1,2,1,32,16,256]{6,4,2,5,0,3,1:T(8,128)(2,1)} %bitcast.15) | data formatting | bytes 8388608 | tf_op jit(solution)/shard_map/transpose | solution.py:43
  89.2 7.2 %reshape_reshape.10 = bf16[8,2,1,32,32,128]{5,4,3,1,0,2:T(8,128)(2,1)} reshape(bf16[8,1,2,1,32,16,256]{6,5,4,2,0,3,1:T(8,128)(2,1)} %copy.68) | data formatting | bytes 8388608 | tf_op jit(solution)/shard_map/reshape;reshape | solution.py:62
  96.4 5.9 %copy.69 = bf16[2,32,1,8,32,128]{5,4,3,1,0,2:T(8,128)(2,1)} copy(bf16[2,32,1,8,32,128]{5,1,4,0,3,2:T(8,128)(2,1)} %bitcast.90) | data formatting | bytes 8388608 | tf_op jit(solution)/shard_map/transpose | solution.py:63
  102.3 10.7 %gather_fusion.3 = bf16[192,256,128]{2,1,0:T(8,128)(2,1)} fusion(bf16[64,1,256,128]{3,2,0,1:T(8,128)(2,1)} %bitcast.84, s32[192]{0:T(256)S(1)} %reshape.181), kind=kCustom, calls=%fused_computation.3 | custom fusion | bytes 25167360 | tf_op jit(solution)/shard_map/gather | solution.py:72
  112.9 13.7 %all-gather.5.cloned.1.call-done = bf16[256,128,128]{2,1,0:T(8,128)(2,1)} async-done(((bf16[16,128,128]{2,1,0:T(8,128)(2,1)}), bf16[256,128,128]{2,1,0:T(8,128)(2,1)}) %all-gather.5.cloned.1.call-update) | async-done | bytes 8388624 | tf_op jit(solution)/shard_map/all_gather | solution.py:36
  126.6 8.3 %gather_fusion.4 = bf16[48,4,128,128]{3,2,1,0:T(8,128)(2,1)} fusion(bf16[64,4,128,128]{3,2,1,0:T(8,128)(2,1)} %bitcast.93, s32[1024]{0:T(1024)S(1)} %pad_clamp_fusion.2), kind=kCustom, calls=%fused_computation.4 | custom fusion | bytes 12583104 | tf_op jit(solution)/shard_map/gather | solution.py:74
  134.9 13.0 %bitcast_select_fusion = f32[48,256,128]{2,1,0:T(8,128)} fusion(pred[48]{0:T(512)(128)(4,1)S(1)} %iota_compare_fusion.1, bf16[48,4,256,128]{3,2,1,0:T(8,128)(2,1)} %bitcast.92, bf16[48,4,128,128]{3,2,1,0:T(8,128)(2,1)} %gather_fusion.4), kind=kOutput, calls=%fused_computation.16 | convolution fusion | flops 1612185600 | bytes 25165872 | tf_op jit(solution)/shard_map/emrc,emcb->erb/dot_general | solution.py:73
  147.9 4.3 %broadcast_in_dim.61 = f32[64,256,128]{2,1,0:T(8,128)} broadcast(f32[]{:T(128)} %constant.21.clone.1), dimensions={} | broadcast | bytes 8388612 | tf_op jit(solution)/shard_map/broadcast_in_dim | solution.py:78
  152.2 15.2 %scatter_fusion = f32[64,256,128]{2,1,0:T(8,128)} fusion(f32[64,256,128]{2,1,0:T(8,128)} %broadcast_in_dim.61, s32[48]{0:T(128)S(1)} %fusion.6, f32[48,256,128]{2,1,0:T(8,128)} %bitcast_select_fusion), kind=kCustom, calls=%fused_computation.5 | custom fusion | flops 1572864 | bytes 18874560 | tf_op jit(solution)/shard_map/scatter-add | solution.py:78
  167.4 4.3 %convert_element_type.31 = bf16[64,256,128]{2,1,0:T(8,128)(2,1)S(1)} convert(f32[64,256,128]{2,1,0:T(8,128)} %scatter_fusion) | non-fusion elementwise | flops 2097152 | bytes 12582912 | tf_op jit(solution)/shard_map/convert_element_type | solution.py:81
  171.7 4.7 %copy.71 = bf16[8,2,1,32,32,128]{5,4,3,1,0,2:T(8,128)(2,1)} copy(bf16[8,2,1,32,32,128]{5,3,0,4,1,2:T(8,128)(2,1)S(1)} %bitcast.86) | data formatting | bytes 8388608 | tf_op jit(solution)/shard_map/transpose | solution.py:84
  176.4 7.2 %reshape_reshape.11 = bf16[8,1,2,1,32,16,256]{6,5,4,2,0,3,1:T(8,128)(2,1)} reshape(bf16[8,2,1,32,32,128]{5,4,3,1,0,2:T(8,128)(2,1)} %copy.71) | data formatting | bytes 8388608 | tf_op jit(solution)/shard_map/reshape;reshape | solution.py:87
  183.6 5.9 %copy.72 = bf16[8,16,1,2,1,32,256]{6,5,3,1,0,4,2:T(8,128)(2,1)} copy(bf16[8,16,1,2,1,32,256]{6,1,5,3,0,4,2:T(8,128)(2,1)} %bitcast.91) | data formatting | bytes 8388608 | tf_op jit(solution)/shard_map/transpose | solution.py:88
  189.4 8.8 %all-to-all-start.1 = ((bf16[128,1,2,1,1,32,256]{6,5,2,4,3,1,0:T(8,128)(2,1)}), bf16[128,1,2,1,1,32,256]{6,5,2,4,3,1,0:T(8,128)(2,1)}, u32[]{:S(2)}, u32[]{:S(2)}) async-start(bf16[128,1,2,1,1,32,256]{6,5,2,4,3,1,0:T(8,128)(2,1)} %bitcast.89), calls=%async_computation.1 | async-start | bytes 8388608 | tf_op jit(solution)/shard_map/all_to_all | solution.py:91
  198.3 1.0 all-gather.3.cloned.1.call-done
  199.3 83.7 %while.10 = (s32[]{:T(128)}, f32[4,8,128,512]{3,2,1,0:T(8,128)}, s32[4]{0:T(128)S(1)}, s32[32,8]{1,0:T(8,128)S(1)}, bf16[256,128,128]{2,1,0:T(8,128)(2,1)}, /*in...) while((s32[]{:T(128)}, f32[4,8,128,512]{3,2,1,0:T(8,128)}, ...), condition=%wide.region_1.2_spmd, body=%wide.region_0.1_spmd.sunk | while | flops 1073744256 | bytes 33566888 | solution.py:60
  199.3 0.6 dynamic_slice.36
  201.8 0.1 reshape.220
  201.9 4.3 %gather_fusion = bf16[64,128,128]{2,1,0:T(8,128)(2,1)S(1)} fusion(bf16[256,128,128]{2,1,0:T(8,128)(2,1)} %get-tuple-element.166, s32[1024]{0:T(1024)S(1)} %pad_clamp_fusion.5), kind=kCustom, calls=%fused_computation.clone.1 | custom fusion | bytes 4194560 | tf_op jit(solution)/shard_map/while/body/eval_jaxpr/gather | solution.py:54
  206.4 0.1 reshape.221
  206.5 7.7 %gather_fusion.1 = bf16[64,128,512]{2,1,0:T(8,128)(2,1)} fusion(bf16[32,128,512]{2,1,0:T(8,128)(2,1)} %get-tuple-element.168, s32[1024]{0:T(1024)S(1)} %pad_clamp_fusion.6), kind=kCustom, calls=%fused_computation.1.clone.1 | custom fusion | bytes 16777472 | tf_op jit(solution)/shard_map/while/body/eval_jaxpr/gather | solution.py:53
  214.2 6.0 %bitcast_dynamic-update-slice_fusion.2 = f32[4,8,128,512]{3,2,1,0:T(8,128)} fusion(f32[4,8,128,512]{3,2,1,0:T(8,128)} %get-tuple-element.153, s32[]{:T(128)S(6)} %copy.88, bf16[8,8,128,128]{3,2,1,0:T(8,128)(2,1)S(1)} %bitcast.83, bf16[8,8,128,512]{3,2,1,0:T(8,128)(2,1)} %bitcast.82), kind=kOutput, calls=%fused_computation.6.clone.1 | convolution fusion | flops 1073741824 | bytes 12582916 | tf_op jit(solution)/shard_map/while/body/eval_jaxpr/akrc,akce->are/dot_general | solution.py:55
  220.2 0.6 dynamic_slice.36
  222.7 0.1 reshape.220
  222.8 4.3 %gather_fusion = bf16[64,128,128]{2,1,0:T(8,128)(2,1)S(1)} fusion(bf16[256,128,128]{2,1,0:T(8,128)(2,1)} %get-tuple-element.166, s32[1024]{0:T(1024)S(1)} %pad_clamp_fusion.5), kind=kCustom, calls=%fused_computation.clone.1 | custom fusion | bytes 4194560 | tf_op jit(solution)/shard_map/while/body/eval_jaxpr/gather | solution.py:54
  227.3 0.1 reshape.221
  227.4 7.7 %gather_fusion.1 = bf16[64,128,512]{2,1,0:T(8,128)(2,1)} fusion(bf16[32,128,512]{2,1,0:T(8,128)(2,1)} %get-tuple-element.168, s32[1024]{0:T(1024)S(1)} %pad_clamp_fusion.6), kind=kCustom, calls=%fused_computation.1.clone.1 | custom fusion | bytes 16777472 | tf_op jit(solution)/shard_map/while/body/eval_jaxpr/gather | solution.py:53
  235.1 6.0 %bitcast_dynamic-update-slice_fusion.2 = f32[4,8,128,512]{3,2,1,0:T(8,128)} fusion(f32[4,8,128,512]{3,2,1,0:T(8,128)} %get-tuple-element.153, s32[]{:T(128)S(6)} %copy.88, bf16[8,8,128,128]{3,2,1,0:T(8,128)(2,1)S(1)} %bitcast.83, bf16[8,8,128,512]{3,2,1,0:T(8,128)(2,1)} %bitcast.82), kind=kOutput, calls=%fused_computation.6.clone.1 | convolution fusion | flops 1073741824 | bytes 12582916 | tf_op jit(solution)/shard_map/while/body/eval_jaxpr/akrc,akce->are/dot_general | solution.py:55
  241.1 0.6 dynamic_slice.36
  243.7 0.1 reshape.220
  243.8 4.3 %gather_fusion = bf16[64,128,128]{2,1,0:T(8,128)(2,1)S(1)} fusion(bf16[256,128,128]{2,1,0:T(8,128)(2,1)} %get-tuple-element.166, s32[1024]{0:T(1024)S(1)} %pad_clamp_fusion.5), kind=kCustom, calls=%fused_computation.clone.1 | custom fusion | bytes 4194560 | tf_op jit(solution)/shard_map/while/body/eval_jaxpr/gather | solution.py:54
  248.2 0.1 reshape.221
  248.3 7.7 %gather_fusion.1 = bf16[64,128,512]{2,1,0:T(8,128)(2,1)} fusion(bf16[32,128,512]{2,1,0:T(8,128)(2,1)} %get-tuple-element.168, s32[1024]{0:T(1024)S(1)} %pad_clamp_fusion.6), kind=kCustom, calls=%fused_computation.1.clone.1 | custom fusion | bytes 16777472 | tf_op jit(solution)/shard_map/while/body/eval_jaxpr/gather | solution.py:53
  256.0 6.0 %bitcast_dynamic-update-slice_fusion.2 = f32[4,8,128,512]{3,2,1,0:T(8,128)} fusion(f32[4,8,128,512]{3,2,1,0:T(8,128)} %get-tuple-element.153, s32[]{:T(128)S(6)} %copy.88, bf16[8,8,128,128]{3,2,1,0:T(8,128)(2,1)S(1)} %bitcast.83, bf16[8,8,128,512]{3,2,1,0:T(8,128)(2,1)} %bitcast.82), kind=kOutput, calls=%fused_computation.6.clone.1 | convolution fusion | flops 1073741824 | bytes 12582916 | tf_op jit(solution)/shard_map/while/body/eval_jaxpr/akrc,akce->are/dot_general | solution.py:55
  262.1 0.6 dynamic_slice.36
  264.7 4.3 %gather_fusion = bf16[64,128,128]{2,1,0:T(8,128)(2,1)S(1)} fusion(bf16[256,128,128]{2,1,0:T(8,128)(2,1)} %get-tuple-element.166, s32[1024]{0:T(1024)S(1)} %pad_clamp_fusion.5), kind=kCustom, calls=%fused_computation.clone.1 | custom fusion | bytes 4194560 | tf_op jit(solution)/shard_map/while/body/eval_jaxpr/gather | solution.py:54
  269.2 0.1 reshape.221
  269.3 7.7 %gather_fusion.1 = bf16[64,128,512]{2,1,0:T(8,128)(2,1)} fusion(bf16[32,128,512]{2,1,0:T(8,128)(2,1)} %get-tuple-element.168, s32[1024]{0:T(1024)S(1)} %pad_clamp_fusion.6), kind=kCustom, calls=%fused_computation.1.clone.1 | custom fusion | bytes 16777472 | tf_op jit(solution)/shard_map/while/body/eval_jaxpr/gather | solution.py:53
  277.0 6.0 %bitcast_dynamic-update-slice_fusion.2 = f32[4,8,128,512]{3,2,1,0:T(8,128)} fusion(f32[4,8,128,512]{3,2,1,0:T(8,128)} %get-tuple-element.153, s32[]{:T(128)S(6)} %copy.88, bf16[8,8,128,128]{3,2,1,0:T(8,128)(2,1)S(1)} %bitcast.83, bf16[8,8,128,512]{3,2,1,0:T(8,128)(2,1)} %bitcast.82), kind=kOutput, calls=%fused_computation.6.clone.1 | convolution fusion | flops 1073741824 | bytes 12582916 | tf_op jit(solution)/shard_map/while/body/eval_jaxpr/akrc,akce->are/dot_general | solution.py:55
  283.0 10.5 %reshape.209 = f32[4096,1,2,256]{3,2,0,1:T(2,128)} reshape(f32[4,8,128,512]{3,2,1,0:T(8,128)} %get-tuple-element.42) | data formatting | bytes 16777216 | tf_op jit(solution)/shard_map/reshape | solution.py:61
  293.5 13.1 %copy.79 = f32[4096,1,2,256]{0,3,2,1:T(8,128)} copy(f32[4096,1,2,256]{3,2,0,1:T(2,128)} %reshape.209) | data formatting | bytes 16777216 | tf_op jit(solution)/shard_map/reshape | solution.py:61
  306.6 6.5 %bitcast_convert_fusion = f32[128,1,1,2,1,1,32,256]{7,6,0,3,5,4,2,1:T(8,128)} fusion(bf16[128,1,2,1,1,32,256]{6,5,2,4,3,1,0:T(8,128)(2,1)} %all-to-all-done.1), kind=kLoop, calls=%fused_computation.17 | loop fusion | flops 2097152 | bytes 12582912 | tf_op jit(solution)/shard_map/convert_element_type | solution.py:109
  313.1 9.0 %copy.75 = f32[1,2,4096,256]{2,3,1,0:T(8,128)} copy(f32[1,2,4096,256]{3,2,1,0:T(8,128)} %bitcast.85) | data formatting | bytes 16777216 | tf_op jit(solution)/shard_map/convert_element_type | solution.py:109
  322.1 11.7 %fusion.2 = bf16[1,2,4096,256]{2,3,1,0:T(8,128)(2,1)} fusion(f32[1,2,4096,256]{2,3,1,0:T(8,128)} %copy.75, f32[4096,1,2,256]{0,3,2,1:T(8,128)} %copy.79, bf16[1,2,4096,256]{2,3,1,0:T(8,128)(2,1)} %copy.63, f32[2]{0:T(128)S(1)} %fusion.5, f32[4096,256]{0,1:T(8,128)} %add_subtract_fusion), kind=kLoop, calls=%fused_computation.15 | loop fusion | flops 12582912 | bytes 29360136 | tf_op jit(solution)/shard_map/convert_element_type | solution.py:110
  333.8 6.3 %copy.76 = bf16[1,2,4096,256]{3,2,1,0:T(8,128)(2,1)} copy(bf16[1,2,4096,256]{2,3,1,0:T(8,128)(2,1)} %fusion.2) | data formatting | bytes 8388608 | tf_op jit(solution)/shard_map/convert_element_type | solution.py:110
  (49 shorter events, 1.0 us)
Async XLA Ops:
  6.5 120.1 %all-gather.5.cloned.1.call-start = ((), (), s32[]{:S(2)}) async-start(), calls=%async_computation.3 | async-start | bytes 8912896 | tf_op jit(solution)/shard_map/all_gather | solution.py:36
  7.3 192.0 %all-gather.3.cloned.1.call-start = ((), (), s32[]{:S(2)}) async-start(), calls=%async_computation.2 | async-start | bytes 8912896 | tf_op jit(solution)/shard_map/all_gather | solution.py:35
  12.9 12.0 %copy-start.3 = (s32[64,4]{0,1:T(4,128)S(1)}, s32[64,4]{0,1:T(4,128)}, u32[]{:S(2)}) copy-start(s32[64,4]{0,1:T(4,128)} %param.21) | copy-start | bytes 3076
  12.9 12.1 %copy-start.6 = (s32[32]{0:T(128)S(1)}, s32[32]{0:T(128)}, u32[]{:S(2)}) copy-start(s32[32]{0:T(128)} %param.23) | copy-start | bytes 388
  12.9 14.1 %copy-start.4 = (s32[256]{0:T(256)S(1)}, s32[256]{0:T(256)}, u32[]{:S(2)}) copy-start(s32[256]{0:T(256)} %param.20) | copy-start | bytes 3076
  12.9 69.2 %all-to-all-start = ((bf16[1,1,2,1,128,32,256]{6,5,2,3,1,0,4:T(8,128)(2,1)}), bf16[1,1,2,1,128,32,256]{6,5,2,3,1,0,4:T(8,128)(2,1)}, u32[]{:S(2)}, u32[]{:S(2)}) async-start(bf16[1,1,2,1,128,32,256]{6,5,2,3,1,0,4:T(8,128)(2,1)} %copy.67), calls=%async_computation | async-start | bytes 8388608 | tf_op jit(solution)/shard_map/all_to_all | solution.py:41
  44.7 6.5 %copy-start.7 = (s32[8]{0:T(128)S(1)}, s32[8]{0:T(128)}, u32[]{:S(2)}) copy-start(s32[8]{0:T(128)} %param.24) | copy-start | bytes 100
  44.7 7.2 %copy-start.1 = (f32[4096]{0:T(1024)S(1)}, f32[4096]{0:T(1024)}, u32[]{:S(2)}) copy-start(f32[4096]{0:T(1024)} %param.27) | copy-start | bytes 49156
  44.7 7.9 %copy-start.2 = (f32[400]{0:T(512)S(1)}, f32[400]{0:T(512)}, u32[]{:S(2)}) copy-start(f32[400]{0:T(512)} %param.26) | copy-start | bytes 4804
  44.7 9.2 %copy-start.5 = (s32[2]{0:T(128)S(1)}, s32[2]{0:T(128)}, u32[]{:S(2)}) copy-start(s32[2]{0:T(128)} %param.25) | copy-start | bytes 28
  189.4 9.9 %copy-start = (s32[32,8]{0,1:T(8,128)S(1)}, s32[32,8]{0,1:T(8,128)}, u32[]{:S(2)}) copy-start(s32[32,8]{0,1:T(8,128)} %param.19) | copy-start | bytes 3076
  189.4 117.2 %all-to-all-start.1 = ((bf16[128,1,2,1,1,32,256]{6,5,2,4,3,1,0:T(8,128)(2,1)}), bf16[128,1,2,1,1,32,256]{6,5,2,4,3,1,0:T(8,128)(2,1)}, u32[]{:S(2)}, u32[]{:S(2)}) async-start(bf16[128,1,2,1,1,32,256]{6,5,2,4,3,1,0:T(8,128)(2,1)} %bitcast.89), calls=%async_computation.1 | async-start | bytes 8388608 | tf_op jit(solution)/shard_map/all_to_all | solution.py:91
Sparse Core Ops, SparseCore 0:
  9.5 117.1 all-gather.4
  128.8 70.4 all-gather.2
where the time goes:
time: 350 us; the launch traced here: 347 us
  local copies, waits for them, and re-layouts  183 us (52%)
  other arithmetic  43.8 us (13%)
  waiting for transfers between devices  40.9 us (12%)
  matrix products  36.9 us (11%)
  starting transfers between devices  20.8 us (6%)
  between operations  13.5 us (4%)
  loops' own time  7.72 us (2%)
    gather x4, local copies, waits for them, and re-layouts, ladder_block(): picked_rows = arranged[screen_part]  30.8 us
    all_to_all x1, waiting for transfers between devices, body(): lax.all_to_all(flat, ('occ', 'vir'), split_axis=4, concat_axis=0, tiled=T...  24.8 us
    dot_general x4, matrix products, ladder_block(): jnp.einsum('akrc,akce->are', weights, picked_rows, preferred_element_type...  24 us
    reshape x2, local copies, waits for them, and re-layouts, body(): total.reshape(width_all, slab_rows, window, block_cols)  23.7 us
    gather x4, local copies, waits for them, and re-layouts, ladder_block(): weights = all_ladder[slot_part]  17.3 us
    scatter-add x1, other arithmetic, body(): jnp.zeros((column_tiles, slab_all * inner, tile_side), jnp.float32)  15.2 us
    all_gather x1, waiting for transfers between devices, body(): lax.all_gather(cycle_tiles, 'vir', axis=0, tiled=True)  13.7 us
    dot_general x1, matrix products, body(): jnp.einsum('emrc,emcb->erb', picked, cycle_sel[columns], preferred_elemen...  13 us
  transfers between devices with their start and end apart: 4, of which 3 were waited for; matrix products, arithmetic and copies ran while one was open for 66% of the time, Pallas kernels for 0%

commit v1 on v0

--- a/solution.py
+++ b/solution.py
@@ -3,6 +3,11 @@
 import jax.numpy as jnp
 from jax import lax
 from jax.sharding import PartitionSpec as P
+
+
+def swapped_in(shard, mesh_axis, dim):
+    sent = jnp.stack([shard] * lax.axis_size(mesh_axis))
+    return jnp.concatenate(lax.all_to_all(sent, mesh_axis, 0, 0), axis=dim)
 
 
 def body(
@@ -33,7 +38,7 @@
     slab_all = slab_rows * occ_count
     all_ladder, all_cycle = (
         lax.all_gather(ladder_tiles, "vir", axis=0, tiled=True),
-        lax.all_gather(cycle_tiles, "vir", axis=0, tiled=True),
+        swapped_in(cycle_tiles, "vir", 0),
     )
     front, inner = (1, rows_here)
     split = amplitudes.reshape(slab_rows, window, front, occ_count, vir_count, inner, block_cols)

time: 350 us -> 543 us (1.55)
  waiting for transfers between devices: 40.9 us -> 207 us
  starting transfers between devices: 20.8 us -> 42.9 us
  local copies, waits for them, and re-layouts: 183 us -> 189 us
    all_to_all x0 -> x1, waiting for transfers between devices: none -> 132 us  [swapped_in(): return jnp.concatenate(lax.all_to_all(sent, mesh_axis, 0, 0), axis=dim)]
    all_to_all x1, waiting for transfers between devices: 24.8 us -> 52.3 us  [body(): lax.all_to_all(flat, ('occ', 'vir'), split_axis=4, concat_axis=0, tiled=T...]
    all_to_all x1, waiting for transfers between devices: 0.01 us -> 22.2 us  [body(): lax.all_to_all(shaped, ('occ', 'vir'), split_axis=0, concat_axis=4, tiled...]
    all_to_all x1, starting transfers between devices: 8.83 us -> 24 us  [body(): lax.all_to_all(shaped, ('occ', 'vir'), split_axis=0, concat_axis=4, tiled...]
    all_gather x1 -> x0, waiting for transfers between devices: 13.7 us -> none  [body(): lax.all_gather(cycle_tiles, 'vir', axis=0, tiled=True)]
    all_to_all x0 -> x1, starting transfers between devices: none -> 6.88 us  [swapped_in(): return jnp.concatenate(lax.all_to_all(sent, mesh_axis, 0, 0), axis=dim)]
    another operation x0 -> x1, local copies, waits for them, and re-layouts: none -> 5.47 us  [swapped_in(): sent = jnp.stack([shard] * lax.axis_size(mesh_axis))]
  transfers between devices with their start and end apart: 4 -> 4, of which waited for: 3 -> 3; matrix products, arithmetic and copies ran while one was open for 66% -> 27% of each run, Pallas kernels for 0% -> 0%
where the time goes in v1:
time: 543 us; the launch traced here: 540 us
  waiting for transfers between devices  207 us (38%)
  local copies, waits for them, and re-layouts  189 us (35%)
  other arithmetic  43.7 us (8%)
  starting transfers between devices  42.9 us (8%)
  matrix products  36.4 us (7%)
  between operations  13.5 us (2%)
  loops' own time  7.86 us (1%)
    all_to_all x1, waiting for transfers between devices, swapped_in(): return jnp.concatenate(lax.all_to_all(sent, mesh_axis, 0, 0), axis=dim)  132 us
    all_to_all x1, waiting for transfers between devices, body(): lax.all_to_all(flat, ('occ', 'vir'), split_axis=4, concat_axis=0, tiled=T...  52.3 us
    gather x4, local copies, waits for them, and re-layouts, ladder_block(): picked_rows = arranged[screen_part]  31.3 us
    all_to_all x1, starting transfers between devices, body(): lax.all_to_all(shaped, ('occ', 'vir'), split_axis=0, concat_axis=4, tiled...  24 us
    dot_general x4, matrix products, ladder_block(): jnp.einsum('akrc,akce->are', weights, picked_rows, preferred_element_type...  24 us
    reshape x2, local copies, waits for them, and re-layouts, body(): total.reshape(width_all, slab_rows, window, block_cols)  23.7 us
    all_to_all x1, waiting for transfers between devices, body(): lax.all_to_all(shaped, ('occ', 'vir'), split_axis=0, concat_axis=4, tiled...  22.2 us
    gather x4, local copies, waits for them, and re-layouts, ladder_block(): weights = all_ladder[slot_part]  17.3 us
  transfers between devices with their start and end apart: 4, of which 3 were waited for; matrix products, arithmetic and copies ran while one was open for 27% of the time, Pallas kernels for 0%

profile of v1, /device:TPU:1, one launch (start us, length us, event | category | flops | bytes accessed | tf_op | source)
XLA Modules:
  0.0 540.0 jit_solution(14434707343452534979)
XLA Ops:
  6.5 4.8 copy.67
  11.4 11.9 %all-to-all-start = ((bf16[1,1,2,1,128,32,256]{6,5,2,3,1,0,4:T(8,128)(2,1)}), bf16[1,1,2,1,128,32,256]{6,5,2,3,1,0,4:T(8,128)(2,1)}, u32[]{:S(2)}, u32[]{:S(2)}) async-start(bf16[1,1,2,1,128,32,256]{6,5,2,3,1,0,4:T(8,128)(2,1)} %copy.67), calls=%async_computation | async-start | bytes 8388608 | tf_op jit(solution)/shard_map/all_to_all | solution.py:46
  23.4 0.7 all-gather.2.cloned.1.call-update
  24.1 52.3 %all-to-all-done = bf16[1,1,2,1,128,32,256]{6,5,2,3,1,0,4:T(8,128)(2,1)} async-done(((bf16[1,1,2,1,128,32,256]{6,5,2,3,1,0,4:T(8,128)(2,1)}), bf16[1,1,2,1,128,32,256]{6,5,2,3,1,0,4:T(8,128)(2,1)}, u32[]{:S(2)}, u32[]{:S(2)}) %all-to-all-start) | async-done | bytes 4194336 | tf_op jit(solution)/shard_map/all_to_all | solution.py:46
  76.3 5.5 %stack.2 = bf16[16,16,128,128]{3,2,1,0:T(8,128)(2,1)} broadcast(bf16[16,128,128]{2,1,0:T(8,128)(2,1)S(1)} %copy-done), dimensions={1,2,3} | broadcast | bytes 8912896 | tf_op jit(solution)/shard_map/stack | solution.py:9
  81.8 6.9 %all-to-all-start.1 = ((bf16[16,16,128,128]{3,2,1,0:T(8,128)(2,1)}), bf16[16,16,128,128]{3,2,1,0:T(8,128)(2,1)}, u32[]{:S(2)}, u32[]{:S(2)}) async-start(bf16[16,16,128,128]{3,2,1,0:T(8,128)(2,1)} %stack.2), calls=%async_computation.1 | async-start | bytes 16777216 | tf_op jit(solution)/shard_map/all_to_all | solution.py:10
  88.7 0.1 copy.70
  88.8 0.6 dynamic_slice.25
  89.4 0.7 fusion.6
  90.1 0.6 gather_fusion.2
  90.7 0.1 reshape.179
  90.8 0.7 iota_compare_fusion.1
  91.5 7.1 %copy.68 = bf16[8,1,2,1,32,16,256]{6,5,4,2,0,3,1:T(8,128)(2,1)} copy(bf16[8,1,2,1,32,16,256]{6,4,2,5,0,3,1:T(8,128)(2,1)} %bitcast.15) | data formatting | bytes 8388608 | tf_op jit(solution)/shard_map/transpose | solution.py:48
  98.6 7.1 %reshape_reshape.13 = bf16[8,2,1,32,32,128]{5,4,3,1,0,2:T(8,128)(2,1)} reshape(bf16[8,1,2,1,32,16,256]{6,5,4,2,0,3,1:T(8,128)(2,1)} %copy.68) | data formatting | bytes 8388608 | tf_op jit(solution)/shard_map/reshape;reshape | solution.py:67
  105.7 5.8 %copy.69 = bf16[2,32,1,8,32,128]{5,4,3,1,0,2:T(8,128)(2,1)} copy(bf16[2,32,1,8,32,128]{5,1,4,0,3,2:T(8,128)(2,1)} %bitcast.90) | data formatting | bytes 8388608 | tf_op jit(solution)/shard_map/transpose | solution.py:68
  111.5 10.6 %gather_fusion.3 = bf16[192,256,128]{2,1,0:T(8,128)(2,1)} fusion(bf16[64,1,256,128]{3,2,0,1:T(8,128)(2,1)} %bitcast.84, s32[192]{0:T(256)S(1)} %reshape.179), kind=kCustom, calls=%fused_computation.3 | custom fusion | bytes 25167360 | tf_op jit(solution)/shard_map/gather | solution.py:77
  122.1 131.5 %all-to-all-done.1 = bf16[16,16,128,128]{3,2,1,0:T(8,128)(2,1)} async-done(((bf16[16,16,128,128]{3,2,1,0:T(8,128)(2,1)}), bf16[16,16,128,128]{3,2,1,0:T(8,128)(2,1)}, u32[]{:S(2)}, u32[]{:S(2)}) %all-to-all-start.1) | async-done | bytes 8388640 | tf_op jit(solution)/shard_map/all_to_all | solution.py:10
  253.7 8.3 %gather_fusion.4 = bf16[48,4,128,128]{3,2,1,0:T(8,128)(2,1)} fusion(bf16[64,4,128,128]{3,2,1,0:T(8,128)(2,1)} %bitcast.20, s32[1024]{0:T(1024)S(1)} %pad_clamp_fusion.2), kind=kCustom, calls=%fused_computation.4 | custom fusion | bytes 12583104 | tf_op jit(solution)/shard_map/gather | solution.py:79
  262.0 12.4 %bitcast_select_fusion = f32[48,256,128]{2,1,0:T(8,128)} fusion(pred[48]{0:T(512)(128)(4,1)S(1)} %iota_compare_fusion.1, bf16[48,4,256,128]{3,2,1,0:T(8,128)(2,1)} %bitcast.92, bf16[48,4,128,128]{3,2,1,0:T(8,128)(2,1)} %gather_fusion.4), kind=kOutput, calls=%fused_computation.16 | convolution fusion | flops 1612185600 | bytes 25165872 | tf_op jit(solution)/shard_map/emrc,emcb->erb/dot_general | solution.py:78
  274.4 4.3 broadcast_in_dim.61
  278.7 15.2 %scatter_fusion = f32[64,256,128]{2,1,0:T(8,128)} fusion(f32[64,256,128]{2,1,0:T(8,128)} %broadcast_in_dim.61, s32[48]{0:T(128)S(1)} %fusion.6, f32[48,256,128]{2,1,0:T(8,128)} %bitcast_select_fusion), kind=kCustom, calls=%fused_computation.5 | custom fusion | flops 1572864 | bytes 18874560 | tf_op jit(solution)/shard_map/scatter-add | solution.py:83
  293.9 4.1 convert_element_type.31
  298.0 4.7 copy.71
  302.7 7.1 %reshape_reshape.15 = bf16[8,1,2,1,32,16,256]{6,5,4,2,0,3,1:T(8,128)(2,1)} reshape(bf16[8,2,1,32,32,128]{5,4,3,1,0,2:T(8,128)(2,1)} %copy.71) | data formatting | bytes 8388608 | tf_op jit(solution)/shard_map/reshape;reshape | solution.py:92
  309.8 5.8 %copy.72 = bf16[8,16,1,2,1,32,256]{6,5,3,1,0,4,2:T(8,128)(2,1)} copy(bf16[8,16,1,2,1,32,256]{6,1,5,3,0,4,2:T(8,128)(2,1)} %bitcast.91) | data formatting | bytes 8388608 | tf_op jit(solution)/shard_map/transpose | solution.py:93
  315.7 24.0 %all-to-all-start.2 = ((bf16[128,1,2,1,1,32,256]{6,5,2,4,3,1,0:T(8,128)(2,1)}), bf16[128,1,2,1,1,32,256]{6,5,2,4,3,1,0:T(8,128)(2,1)}, u32[]{:S(2)}, u32[]{:S(2)}) async-start(bf16[128,1,2,1,1,32,256]{6,5,2,4,3,1,0:T(8,128)(2,1)} %bitcast.89), calls=%async_computation.2 | async-start | bytes 8388608 | tf_op jit(solution)/shard_map/all_to_all | solution.py:96
  339.7 0.1 reshape.146
  339.8 10.2 %copy.64 = bf16[4096,1,2,256]{3,2,0,1:T(2,128)(2,1)} copy(bf16[4096,1,2,256]{3,0,2,1:T(8,128)(2,1)} %bitcast.88) | data formatting | bytes 8388608 | tf_op jit(solution)/shard_map/transpose | solution.py:51
  349.9 7.7 %reshape.147 = bf16[32,128,512]{2,1,0:T(8,128)(2,1)} reshape(bf16[4096,1,2,256]{3,2,0,1:T(2,128)(2,1)} %copy.64) | data formatting | bytes 8388608 | tf_op jit(solution)/shard_map/reshape | solution.py:51
  357.6 6.5 %copy.63 = bf16[1,2,4096,256]{2,3,1,0:T(8,128)(2,1)} copy(bf16[1,2,4096,256]{3,2,1,0:T(8,128)(2,1)} %param.16) | data formatting | bytes 8388608 | tf_op args[1]
  364.1 0.6 dynamic_slice.27
  364.8 1.2 select_reduce_fusion
  366.0 0.2 fusion.5
  366.2 3.2 add_subtract_fusion
  369.3 22.2 %all-to-all-done.2 = bf16[128,1,2,1,1,32,256]{6,5,2,4,3,1,0:T(8,128)(2,1)} async-done(((bf16[128,1,2,1,1,32,256]{6,5,2,4,3,1,0:T(8,128)(2,1)}), bf16[128,1,2,1,1,32,256]{6,5,2,4,3,1,0:T(8,128)(2,1)}, u32[]{:S(2)}, u32[]{:S(2)}) %all-to-all-start.2) | async-done | bytes 4194336 | tf_op jit(solution)/shard_map/all_to_all | solution.py:96
  391.6 6.6 %bitcast_convert_fusion = f32[128,1,1,2,1,1,32,256]{7,6,0,3,5,4,2,1:T(8,128)} fusion(bf16[128,1,2,1,1,32,256]{6,5,2,4,3,1,0:T(8,128)(2,1)} %all-to-all-done.2), kind=kLoop, calls=%fused_computation.17 | loop fusion | flops 2097152 | bytes 12582912 | tf_op jit(solution)/shard_map/convert_element_type | solution.py:114
  398.2 9.0 %copy.75 = f32[1,2,4096,256]{2,3,1,0:T(8,128)} copy(f32[1,2,4096,256]{3,2,1,0:T(8,128)} %bitcast.85) | data formatting | bytes 16777216 | tf_op jit(solution)/shard_map/convert_element_type | solution.py:114
  407.2 84.2 %while.10 = (s32[]{:T(128)}, f32[4,8,128,512]{3,2,1,0:T(8,128)}, s32[4]{0:T(128)S(1)}, s32[32,8]{1,0:T(8,128)S(1)}, bf16[256,128,128]{2,1,0:T(8,128)(2,1)}, /*in...) while((s32[]{:T(128)}, f32[4,8,128,512]{3,2,1,0:T(8,128)}, ...), condition=%wide.region_1.2_spmd, body=%wide.region_0.1_spmd.sunk | while | flops 1073744256 | bytes 33566888 | solution.py:65
  407.2 0.6 dynamic_slice.36
  409.7 0.1 reshape.218
  409.8 4.3 gather_fusion
  414.3 0.1 reshape.219
  414.4 7.8 %gather_fusion.1 = bf16[64,128,512]{2,1,0:T(8,128)(2,1)} fusion(bf16[32,128,512]{2,1,0:T(8,128)(2,1)} %get-tuple-element.168, s32[1024]{0:T(1024)S(1)} %pad_clamp_fusion.6), kind=kCustom, calls=%fused_computation.1.clone.1 | custom fusion | bytes 16777472 | tf_op jit(solution)/shard_map/while/body/eval_jaxpr/gather | solution.py:58
  422.2 6.0 %bitcast_dynamic-update-slice_fusion.2 = f32[4,8,128,512]{3,2,1,0:T(8,128)} fusion(f32[4,8,128,512]{3,2,1,0:T(8,128)} %get-tuple-element.153, s32[]{:T(128)S(6)} %copy.88, bf16[8,8,128,128]{3,2,1,0:T(8,128)(2,1)S(1)} %bitcast.83, bf16[8,8,128,512]{3,2,1,0:T(8,128)(2,1)} %bitcast.82), kind=kOutput, calls=%fused_computation.6.clone.1 | convolution fusion | flops 1073741824 | bytes 12582916 | tf_op jit(solution)/shard_map/while/body/eval_jaxpr/akrc,akce->are/dot_general | solution.py:60
  428.2 0.6 dynamic_slice.36
  430.8 0.1 reshape.218
  430.9 4.3 gather_fusion
  435.4 0.1 reshape.219
  435.5 7.8 %gather_fusion.1 = bf16[64,128,512]{2,1,0:T(8,128)(2,1)} fusion(bf16[32,128,512]{2,1,0:T(8,128)(2,1)} %get-tuple-element.168, s32[1024]{0:T(1024)S(1)} %pad_clamp_fusion.6), kind=kCustom, calls=%fused_computation.1.clone.1 | custom fusion | bytes 16777472 | tf_op jit(solution)/shard_map/while/body/eval_jaxpr/gather | solution.py:58
  443.3 6.0 %bitcast_dynamic-update-slice_fusion.2 = f32[4,8,128,512]{3,2,1,0:T(8,128)} fusion(f32[4,8,128,512]{3,2,1,0:T(8,128)} %get-tuple-element.153, s32[]{:T(128)S(6)} %copy.88, bf16[8,8,128,128]{3,2,1,0:T(8,128)(2,1)S(1)} %bitcast.83, bf16[8,8,128,512]{3,2,1,0:T(8,128)(2,1)} %bitcast.82), kind=kOutput, calls=%fused_computation.6.clone.1 | convolution fusion | flops 1073741824 | bytes 12582916 | tf_op jit(solution)/shard_map/while/body/eval_jaxpr/akrc,akce->are/dot_general | solution.py:60
  449.3 0.6 dynamic_slice.36
  451.9 4.3 gather_fusion
  456.4 0.1 reshape.219
  456.5 7.8 %gather_fusion.1 = bf16[64,128,512]{2,1,0:T(8,128)(2,1)} fusion(bf16[32,128,512]{2,1,0:T(8,128)(2,1)} %get-tuple-element.168, s32[1024]{0:T(1024)S(1)} %pad_clamp_fusion.6), kind=kCustom, calls=%fused_computation.1.clone.1 | custom fusion | bytes 16777472 | tf_op jit(solution)/shard_map/while/body/eval_jaxpr/gather | solution.py:58
  464.3 6.0 %bitcast_dynamic-update-slice_fusion.2 = f32[4,8,128,512]{3,2,1,0:T(8,128)} fusion(f32[4,8,128,512]{3,2,1,0:T(8,128)} %get-tuple-element.153, s32[]{:T(128)S(6)} %copy.88, bf16[8,8,128,128]{3,2,1,0:T(8,128)(2,1)S(1)} %bitcast.83, bf16[8,8,128,512]{3,2,1,0:T(8,128)(2,1)} %bitcast.82), kind=kOutput, calls=%fused_computation.6.clone.1 | convolution fusion | flops 1073741824 | bytes 12582916 | tf_op jit(solution)/shard_map/while/body/eval_jaxpr/akrc,akce->are/dot_general | solution.py:60
  470.3 0.6 dynamic_slice.36
  473.0 4.3 gather_fusion
  477.5 0.1 reshape.219
  477.6 7.9 %gather_fusion.1 = bf16[64,128,512]{2,1,0:T(8,128)(2,1)} fusion(bf16[32,128,512]{2,1,0:T(8,128)(2,1)} %get-tuple-element.168, s32[1024]{0:T(1024)S(1)} %pad_clamp_fusion.6), kind=kCustom, calls=%fused_computation.1.clone.1 | custom fusion | bytes 16777472 | tf_op jit(solution)/shard_map/while/body/eval_jaxpr/gather | solution.py:58
  485.4 6.0 %bitcast_dynamic-update-slice_fusion.2 = f32[4,8,128,512]{3,2,1,0:T(8,128)} fusion(f32[4,8,128,512]{3,2,1,0:T(8,128)} %get-tuple-element.153, s32[]{:T(128)S(6)} %copy.88, bf16[8,8,128,128]{3,2,1,0:T(8,128)(2,1)S(1)} %bitcast.83, bf16[8,8,128,512]{3,2,1,0:T(8,128)(2,1)} %bitcast.82), kind=kOutput, calls=%fused_computation.6.clone.1 | convolution fusion | flops 1073741824 | bytes 12582916 | tf_op jit(solution)/shard_map/while/body/eval_jaxpr/akrc,akce->are/dot_general | solution.py:60
  491.4 10.6 %reshape.207 = f32[4096,1,2,256]{3,2,0,1:T(2,128)} reshape(f32[4,8,128,512]{3,2,1,0:T(8,128)} %get-tuple-element.42) | data formatting | bytes 16777216 | tf_op jit(solution)/shard_map/reshape | solution.py:66
  502.0 13.2 %copy.79 = f32[4096,1,2,256]{0,3,2,1:T(8,128)} copy(f32[4096,1,2,256]{3,2,0,1:T(2,128)} %reshape.207) | data formatting | bytes 16777216 | tf_op jit(solution)/shard_map/reshape | solution.py:66
  515.2 11.6 %fusion.2 = bf16[1,2,4096,256]{2,3,1,0:T(8,128)(2,1)} fusion(f32[1,2,4096,256]{2,3,1,0:T(8,128)} %copy.75, f32[4096,1,2,256]{0,3,2,1:T(8,128)} %copy.79, bf16[1,2,4096,256]{2,3,1,0:T(8,128)(2,1)} %copy.63, f32[2]{0:T(128)S(1)} %fusion.5, f32[4096,256]{0,1:T(8,128)} %add_subtract_fusion), kind=kLoop, calls=%fused_computation.15 | loop fusion | flops 12582912 | bytes 29360136 | tf_op jit(solution)/shard_map/convert_element_type | solution.py:115
  526.8 6.3 %copy.76 = bf16[1,2,4096,256]{3,2,1,0:T(8,128)(2,1)} copy(bf16[1,2,4096,256]{2,3,1,0:T(8,128)(2,1)} %fusion.2) | data formatting | bytes 8388608 | tf_op jit(solution)/shard_map/convert_element_type | solution.py:115
  (51 shorter events, 1.1 us)
Async XLA Ops:
  11.4 65.0 %copy-start = (bf16[16,128,128]{2,1,0:T(8,128)(2,1)S(1)}, bf16[16,128,128]{2,1,0:T(8,128)(2,1)}, u32[]{:S(2)}) copy-start(bf16[16,128,128]{2,1,0:T(8,128)(2,1)} %param.18) | copy-start | bytes 1572868
  11.4 65.0 %all-to-all-start = ((bf16[1,1,2,1,128,32,256]{6,5,2,3,1,0,4:T(8,128)(2,1)}), bf16[1,1,2,1,128,32,256]{6,5,2,3,1,0,4:T(8,128)(2,1)}, u32[]{:S(2)}, u32[]{:S(2)}) async-start(bf16[1,1,2,1,128,32,256]{6,5,2,3,1,0,4:T(8,128)(2,1)} %copy.67), calls=%async_computation | async-start | bytes 8388608 | tf_op jit(solution)/shard_map/all_to_all | solution.py:46
  23.3 383.8 %all-gather.2.cloned.1.call-start = ((), (), s32[]{:S(2)}) async-start(), calls=%async_computation.3 | async-start | bytes 8912896 | tf_op jit(solution)/shard_map/all_gather | solution.py:40
  81.8 6.9 %copy-start.4 = (s32[64,4]{0,1:T(4,128)S(1)}, s32[64,4]{0,1:T(4,128)}, u32[]{:S(2)}) copy-start(s32[64,4]{0,1:T(4,128)} %param.21) | copy-start | bytes 3076
  81.8 7.0 %copy-start.7 = (s32[32]{0:T(128)S(1)}, s32[32]{0:T(128)}, u32[]{:S(2)}) copy-start(s32[32]{0:T(128)} %param.23) | copy-start | bytes 388
  81.8 171.8 %all-to-all-start.1 = ((bf16[16,16,128,128]{3,2,1,0:T(8,128)(2,1)}), bf16[16,16,128,128]{3,2,1,0:T(8,128)(2,1)}, u32[]{:S(2)}, u32[]{:S(2)}) async-start(bf16[16,16,128,128]{3,2,1,0:T(8,128)(2,1)} %stack.2), calls=%async_computation.1 | async-start | bytes 16777216 | tf_op jit(solution)/shard_map/all_to_all | solution.py:10
  315.7 24.0 %copy-start.5 = (s32[256]{0:T(256)S(1)}, s32[256]{0:T(256)}, u32[]{:S(2)}) copy-start(s32[256]{0:T(256)} %param.20) | copy-start | bytes 3076
  315.7 75.9 %all-to-all-start.2 = ((bf16[128,1,2,1,1,32,256]{6,5,2,4,3,1,0:T(8,128)(2,1)}), bf16[128,1,2,1,1,32,256]{6,5,2,4,3,1,0:T(8,128)(2,1)}, u32[]{:S(2)}, u32[]{:S(2)}) async-start(bf16[128,1,2,1,1,32,256]{6,5,2,4,3,1,0:T(8,128)(2,1)} %bitcast.89), calls=%async_computation.2 | async-start | bytes 8388608 | tf_op jit(solution)/shard_map/all_to_all | solution.py:96
  357.6 6.5 %copy-start.8 = (s32[8]{0:T(128)S(1)}, s32[8]{0:T(128)}, u32[]{:S(2)}) copy-start(s32[8]{0:T(128)} %param.24) | copy-start | bytes 100
  357.6 7.1 %copy-start.2 = (f32[4096]{0:T(1024)S(1)}, f32[4096]{0:T(1024)}, u32[]{:S(2)}) copy-start(f32[4096]{0:T(1024)} %param.27) | copy-start | bytes 49156
  357.6 7.2 %copy-start.3 = (f32[400]{0:T(512)S(1)}, f32[400]{0:T(512)}, u32[]{:S(2)}) copy-start(f32[400]{0:T(512)} %param.26) | copy-start | bytes 4804
  357.6 8.4 %copy-start.6 = (s32[2]{0:T(128)S(1)}, s32[2]{0:T(128)}, u32[]{:S(2)}) copy-start(s32[2]{0:T(128)} %param.25) | copy-start | bytes 28
  398.2 9.0 %copy-start.1 = (s32[32,8]{0,1:T(8,128)S(1)}, s32[32,8]{0,1:T(8,128)}, u32[]{:S(2)}) copy-start(s32[32,8]{0,1:T(8,128)} %param.19) | copy-start | bytes 3076
Sparse Core Ops, SparseCore 0:
  26.3 193.0 all-gather.1
